TPU v7x, 512 devices: a whole 4x8x8 slice. The times are simulated.
512 devices in a mesh: dp: 4 (over x), expert: 128 (over z, y, core).
Axes of the slice: x: 4, y: 8, z: 8, core: 2. Of those that a mesh axis runs over, the one named last changes fastest.
Arguments:
- tokens: bfloat16 [2048, 2048], P('expert', 'dp'), may hold values from -6 to 6
- cotangent: bfloat16 [2048, 2048], P('expert', 'dp'), may hold values from -6 to 6
- expert_ids: int32 [2048, 8], P('expert'), may hold values from 0 to 127, all different within a row; in each aligned block of 16 rows (0 to 15, 16 to 31, ...) at most 2 rows name the same one
- gate_probs: float32 [2048, 8], P('expert'), may hold values from 0.05 to 1
- w_gate: bfloat16 [128, 768, 2048], P('expert', None, 'dp'), may hold values from -0.125 to 0.125
- w_up: bfloat16 [128, 768, 2048], P('expert', None, 'dp'), may hold values from -0.125 to 0.125
- w_down: bfloat16 [128, 768, 2048], P('expert', None, 'dp'), may hold values from -0.21875 to 0.21875
Outputs:
- mixed: bfloat16 [2048, 2048], P('expert', 'dp')
- grad_tokens: bfloat16 [2048, 2048], P('expert', 'dp')
- grad_gate: bfloat16 [128, 768, 2048], P('expert', None, 'dp')
- grad_up: bfloat16 [128, 768, 2048], P('expert', None, 'dp')
- grad_down: bfloat16 [128, 768, 2048], P('expert', None, 'dp')
Inputs may be any that keep to these rules, and one draw needn't show every extreme that they name: `expert_ids`: each token names 8 different experts. The 16 tokens of one index of expert (rows b * 16 to (b + 1) * 16 - 1) name no expert more than 2 times, a bound that some block reaches.
All inputs are finite; a program needn't handle non-finite values.
Results may differ from a plain program's by a relative error of at most 0.02.
Values may be sent and summed in bfloat16 or wider, within the bound.
A program may use at most 64 MiB of HBM per device.

v0:
```python
import jax
import jax.numpy as jnp
from jax import lax
from jax.sharding import PartitionSpec as P


def activate(pre_gate, pre_up, back_hidden):
    sigmas = jax.nn.sigmoid(pre_gate)
    silu_vals = pre_gate * sigmas
    hidden = (silu_vals * pre_up).astype(jnp.bfloat16)
    back_gate = (back_hidden * pre_up * sigmas * (1.0 + pre_gate * (1.0 - sigmas))).astype(
        jnp.bfloat16
    )
    back_up = (back_hidden * silu_vals).astype(jnp.bfloat16)
    return (hidden, back_gate, back_up)


def deliver(outbound):
    return lax.all_to_all(outbound, "expert", split_axis=0, concat_axis=0, tiled=True)


def on_device(tokens, cotangent, expert_ids, gate_probs, w_gate, w_up, w_down):
    tok_rows, columns = tokens.shape
    top_count = expert_ids.shape[1]
    experts = lax.axis_size("expert")
    capacity = min(tok_rows, max(2, 2 * tok_rows * top_count // experts))
    slot_count = experts * capacity
    flat_ids = expert_ids.reshape(-1)
    onehot = (flat_ids[:, None] == jnp.arange(experts, dtype=jnp.int32)[None, :]).astype(jnp.int32)
    before = jnp.cumsum(onehot, axis=0) - onehot
    ranks = jnp.sum(before * onehot, axis=1)
    slot_ids = flat_ids * capacity + ranks
    chosen = (slot_ids[:, None] == jnp.arange(slot_count, dtype=jnp.int32)[None, :]).astype(
        jnp.float32
    )
    chosen = chosen.reshape(tok_rows, top_count, slot_count)
    select = jnp.sum(chosen, axis=1)
    weighted = jnp.sum(chosen * gate_probs[:, :, None], axis=1)
    contract_rows = (((0,), (0,)), ((), ()))
    contract_cols = (((1,), (1,)), ((), ()))
    x_rows = lax.dot_general(
        select.astype(jnp.bfloat16), tokens, contract_rows, preferred_element_type=jnp.float32
    ).astype(jnp.bfloat16)
    back_row = lax.dot_general(
        weighted,
        cotangent.astype(jnp.float32),
        contract_rows,
        precision=lax.Precision.HIGHEST,
        preferred_element_type=jnp.float32,
    ).astype(jnp.bfloat16)
    outbound = jnp.stack([x_rows, back_row], axis=1).reshape(experts, capacity, 2, columns)
    inbound = deliver(outbound).reshape(slot_count, 2, columns)
    x_in = inbound[:, 0]
    d_in = inbound[:, 1]
    gate_mat = w_gate[0]
    up_mat = w_up[0]
    down_mat = w_down[0]
    part_gate = lax.dot_general(x_in, gate_mat, contract_cols, preferred_element_type=jnp.float32)
    part_up = lax.dot_general(x_in, up_mat, contract_cols, preferred_element_type=jnp.float32)
    part_back = lax.dot_general(d_in, down_mat, contract_cols, preferred_element_type=jnp.float32)
    pre_gate, pre_up, back_hidden = (
        lax.psum(part_gate.astype(jnp.bfloat16), "dp").astype(jnp.float32),
        lax.psum(part_up.astype(jnp.bfloat16), "dp").astype(jnp.float32),
        lax.psum(part_back.astype(jnp.bfloat16), "dp").astype(jnp.float32),
    )
    hidden, back_gate, back_up = activate(pre_gate, pre_up, back_hidden)
    expert_out = jnp.dot(hidden, down_mat, preferred_element_type=jnp.float32).astype(jnp.bfloat16)
    back_rows = (
        jnp.dot(back_gate, gate_mat, preferred_element_type=jnp.float32)
        + jnp.dot(back_up, up_mat, preferred_element_type=jnp.float32)
    ).astype(jnp.bfloat16)
    grad_gate = lax.dot_general(
        back_gate, x_in, contract_rows, preferred_element_type=jnp.float32
    ).astype(jnp.bfloat16)
    grad_up = lax.dot_general(
        back_up, x_in, contract_rows, preferred_element_type=jnp.float32
    ).astype(jnp.bfloat16)
    grad_down = lax.dot_general(
        hidden, d_in, contract_rows, preferred_element_type=jnp.float32
    ).astype(jnp.bfloat16)
    homeward = jnp.stack([expert_out, back_rows], axis=1).reshape(experts, capacity, 2, columns)
    returned = deliver(homeward).reshape(slot_count, 2, columns)
    mixed = jnp.dot(
        weighted,
        returned[:, 0].astype(jnp.float32),
        precision=lax.Precision.HIGHEST,
        preferred_element_type=jnp.float32,
    ).astype(jnp.bfloat16)
    grad_tokens = jnp.dot(
        select.astype(jnp.bfloat16), returned[:, 1], preferred_element_type=jnp.float32
    ).astype(jnp.bfloat16)
    return (mixed, grad_tokens, grad_gate[None], grad_up[None], grad_down[None])


def solution(mesh):
    in_specs = (
        P("expert", "dp"),
        P("expert", "dp"),
        P("expert", None),
        P("expert", None),
        P("expert", None, "dp"),
        P("expert", None, "dp"),
        P("expert", None, "dp"),
    )
    out_specs = (
        P("expert", "dp"),
        P("expert", "dp"),
        P("expert", None, "dp"),
        P("expert", None, "dp"),
        P("expert", None, "dp"),
    )
    return jax.shard_map(
        on_device, mesh=mesh, in_specs=in_specs, out_specs=out_specs, check_vma=False
    )
```

profile of v0, /device:TPU:1, one launch (start us, length us, event | category | flops | bytes accessed | tf_op | source)
XLA Modules:
  0.0 158.1 jit_solution(7407230537476773871)
XLA Ops:
  7.2 0.8 copy.34
  8.1 0.8 copy.36
  9.0 0.2 reduce_window_sum.11
  9.2 0.2 select_reduce_fusion.1
  9.4 0.2 convert_reduce_fusion
  9.6 1.0 convolution_convert_fusion.7
  10.7 0.4 convolution_convert_fusion.6
  11.2 0.7 pad_maximum_fusion
  11.9 38.8 %all_to_all.10 = bf16[128,2,2,512]{3,1,2,0:T(2,128)(2,1)S(1)} all-to-all(bf16[128,2,2,512]{3,1,2,0:T(2,128)(2,1)S(1)} %pad_maximum_fusion), channel_id=1, replica_groups=mesh['dp'=4,'expert'=128] {'expert'}, dimensions={0} | all-to-all | bytes 1048576 | tf_op jit(solution)/shard_map/all_to_all | solution.py:19
  50.7 0.4 copy.39
  51.1 0.7 fusion.40
  51.9 1.1 copy-done.2
  53.0 1.1 convolution_convert_fusion.4
  54.1 1.1 convolution_convert_fusion.5
  55.3 1.2 convolution_convert_fusion.3
  56.5 48.8 %all-reduce.3.cloned.1.call-done = (bf16[256,768]{1,0:T(8,128)(2,1)}, bf16[256,768]{1,0:T(8,128)(2,1)}, bf16[256,768]{1,0:T(8,128)(2,1)}) async-done(((bf16[256,768]{1,0:T(8,128)(2,1)}, bf16[256,768]{1,0:T(8,128)(2,1)}, bf16[256,768]{1,0:T(8,128)(2,1)}), (bf16[256,768]{1,0:T(8,128)(2,1)}, bf16[256,768]{1,0:T(8,128)(2,1)}, bf16[256,768]{1,0:T(8,128)(2,1)})) %all-reduce.3.cloned.1.call-update) | async-done | bytes 1179664 | tf_op jit(solution)/shard_map/psum | solution.py:63
  105.2 2.3 %convolution_convert_fusion.8 = bf16[256,512]{1,0:T(8,128)(2,1)} fusion(bf16[1,768,512]{2,1,0:T(8,128)(2,1)S(1)} %copy-done, bf16[256,768]{1,0:T(8,128)(2,1)} %get-tuple-element.7, bf16[256,768]{1,0:T(8,128)(2,1)} %get-tuple-element.9), kind=kOutput, calls=%fused_computation.13 | convolution fusion | flops 203030528 | bytes 1835008 | tf_op jit(solution)/shard_map/dot_general | solution.py:67
  107.6 0.4 fusion.7
  108.0 1.1 stack.21
  109.0 0.4 fusion.17
  109.4 0.7 copy-done.3
  110.4 0.4 fusion.3
  110.9 1.5 pad_maximum_fusion.1
  112.4 15.5 %all-to-all-start.1 = ((bf16[128,2,2,512]{3,1,2,0:T(2,128)(2,1)}), bf16[128,2,2,512]{3,1,2,0:T(2,128)(2,1)S(1)}, u32[]{:S(2)}, u32[]{:S(2)}) async-start(bf16[128,2,2,512]{3,1,2,0:T(2,128)(2,1)} %pad_maximum_fusion.1), calls=%async_computation.1 | async-start | bytes 1048576 | tf_op jit(solution)/shard_map/all_to_all | solution.py:19
  127.9 1.3 fusion
  129.2 1.3 fusion.1
  130.5 1.4 fusion.2
  131.9 16.5 %all-to-all-done.1 = bf16[128,2,2,512]{3,1,2,0:T(2,128)(2,1)S(1)} async-done(((bf16[128,2,2,512]{3,1,2,0:T(2,128)(2,1)}), bf16[128,2,2,512]{3,1,2,0:T(2,128)(2,1)S(1)}, u32[]{:S(2)}, u32[]{:S(2)}) %all-to-all-start.1) | async-done | bytes 524320 | tf_op jit(solution)/shard_map/all_to_all | solution.py:19
  148.5 0.4 copy.42
  148.9 0.7 fusion.39
  149.6 0.8 convolution_convert_fusion.9
  150.4 0.8 convolution_convert_fusion.10
  (32 shorter events, 0.9 us)
Async XLA Ops:
  7.2 48.1 %copy-start = (bf16[1,768,512]{2,1,0:T(8,128)(2,1)S(1)}, bf16[1,768,512]{2,1,0:T(8,128)(2,1)}, u32[]{:S(2)}) copy-start(bf16[1,768,512]{2,1,0:T(8,128)(2,1)} %param.13) | copy-start | bytes 2359300
  7.2 3.5 %copy-start.11 = (bf16[16,512]{1,0:T(8,128)(2,1)S(1)}, bf16[16,512]{1,0:T(8,128)(2,1)}, u32[]{:S(2)}) copy-start(bf16[16,512]{1,0:T(8,128)(2,1)} %param.8) | copy-start | bytes 49156
  7.2 98.0 %all-reduce.3.cloned.1.call-start = ((), (), s32[]{:S(2)}) async-start(), calls=%async_computation.2 | async-start | bytes 2359296 | tf_op jit(solution)/shard_map/psum | solution.py:63
  51.9 1.1 copy-start.2
  53.0 1.1 copy-start.1
  105.2 2.4 %copy-start.4 = (bf16[256,768]{1,0:T(8,128)(2,1)S(1)}, bf16[256,768]{1,0:T(8,128)(2,1)}, u32[]{:S(2)}) copy-start(bf16[256,768]{1,0:T(8,128)(2,1)} %get-tuple-element.7) | copy-start | bytes 1179652
  105.2 2.4 %copy-start.5 = (bf16[256,768]{1,0:T(8,128)(2,1)S(1)}, bf16[256,768]{1,0:T(8,128)(2,1)}, u32[]{:S(2)}) copy-start(bf16[256,768]{1,0:T(8,128)(2,1)} %get-tuple-element.9) | copy-start | bytes 1179652
  105.2 2.4 %copy-start.8 = (bf16[256,768]{1,0:T(8,128)(2,1)S(1)}, bf16[256,768]{1,0:T(8,128)(2,1)}, u32[]{:S(2)}) copy-start(bf16[256,768]{1,0:T(8,128)(2,1)} %get-tuple-element.8) | copy-start | bytes 1179652
  109.0 1.1 copy-start.3
  109.0 1.2 copy-start.6
  109.0 1.3 copy-start.9
  112.4 36.1 %all-to-all-start.1 = ((bf16[128,2,2,512]{3,1,2,0:T(2,128)(2,1)}), bf16[128,2,2,512]{3,1,2,0:T(2,128)(2,1)S(1)}, u32[]{:S(2)}, u32[]{:S(2)}) async-start(bf16[128,2,2,512]{3,1,2,0:T(2,128)(2,1)} %pad_maximum_fusion.1), calls=%async_computation.1 | async-start | bytes 1048576 | tf_op jit(solution)/shard_map/all_to_all | solution.py:19
  127.9 1.3 copy-start.7
  127.9 1.3 copy-start.10
Sparse Core Ops, SparseCore 0:
  56.6 48.5 all-reduce.2
where the time goes:
time: 158 us
  waiting for transfers between devices  65.3 us (41%)
  blocking collectives  38.8 us (25%)
  starting transfers between devices  15.6 us (10%)
  between operations  14.2 us (9%)
  matrix products  13.5 us (9%)
  local copies, waits for them, and re-layouts  7.51 us (5%)
  other arithmetic  3.1 us (2%)
    psum x1, waiting for transfers between devices, on_device(): lax.psum(part_up.astype(jnp.bfloat16), 'dp').astype(jnp.float32)  48.8 us
    all_to_all x1, blocking collectives, deliver(): lax.all_to_all(outbound, 'expert', split_axis=0, concat_axis=0, tiled=True)  38.8 us
    all_to_all x1, waiting for transfers between devices, deliver(): lax.all_to_all(outbound, 'expert', split_axis=0, concat_axis=0, tiled=True)  16.5 us
    all_to_all x1, starting transfers between devices, deliver(): lax.all_to_all(outbound, 'expert', split_axis=0, concat_axis=0, tiled=True)  15.5 us
    unnamed x27, local copies, waits for them, and re-layouts  3.7 us
  transfers between devices with their start and end apart: 2, of which 2 were waited for; matrix products, arithmetic and copies ran while one was open for 3% of the time, Pallas kernels for 0%

commit v1 on v0

--- a/solution.py
+++ b/solution.py
@@ -2,6 +2,7 @@
 import jax.numpy as jnp
 from jax import lax
 from jax.sharding import PartitionSpec as P
+from jax.lax import all_gather
 
 
 def activate(pre_gate, pre_up, back_hidden):
@@ -20,6 +21,10 @@
 
 
 def on_device(tokens, cotangent, expert_ids, gate_probs, w_gate, w_up, w_down):
+
+    def wait_points(mat):
+        return jnp.sum(all_gather(mat, "dp"), axis=0)
+
     tok_rows, columns = tokens.shape
     top_count = expert_ids.shape[1]
     experts = lax.axis_size("expert")
@@ -60,7 +65,7 @@
     part_back = lax.dot_general(d_in, down_mat, contract_cols, preferred_element_type=jnp.float32)
     pre_gate, pre_up, back_hidden = (
         lax.psum(part_gate.astype(jnp.bfloat16), "dp").astype(jnp.float32),
-        lax.psum(part_up.astype(jnp.bfloat16), "dp").astype(jnp.float32),
+        wait_points(part_up.astype(jnp.bfloat16)).astype(jnp.float32),
         lax.psum(part_back.astype(jnp.bfloat16), "dp").astype(jnp.float32),
     )
     hidden, back_gate, back_up = activate(pre_gate, pre_up, back_hidden)

time: 158 us -> 189 us (1.20)
  waiting for transfers between devices: 65.3 us -> 91.9 us
    all_gather x0 -> x1, waiting for transfers between devices: none -> 21.8 us  [wait_points(): return jnp.sum(all_gather(mat, 'dp'), axis=0)]
    psum x1, waiting for transfers between devices: 48.8 us -> 54.6 us  [on_device(): lax.psum(part_back.astype(jnp.bfloat16), 'dp').astype(jnp.float32)]
  transfers between devices with their start and end apart: 2 -> 3, of which waited for: 2 -> 3; matrix products, arithmetic and copies ran while one was open for 3% -> 5% of each run, Pallas kernels for 0% -> 0%
where the time goes in v1:
time: 189 us; the launch traced here: 188 us
  waiting for transfers between devices  91.9 us (49%)
  blocking collectives  38.8 us (21%)
  starting transfers between devices  16.3 us (9%)
  matrix products  15.3 us (8%)
  between operations  14.2 us (8%)
  local copies, waits for them, and re-layouts  6.76 us (4%)
  other arithmetic  4.9 us (3%)
    psum x1, waiting for transfers between devices, on_device(): lax.psum(part_back.astype(jnp.bfloat16), 'dp').astype(jnp.float32)  54.6 us
    all_to_all x1, blocking collectives, deliver(): lax.all_to_all(outbound, 'expert', split_axis=0, concat_axis=0, tiled=True)  38.8 us
    all_gather x1, waiting for transfers between devices, wait_points(): return jnp.sum(all_gather(mat, 'dp'), axis=0)  21.8 us
    all_to_all x1, starting transfers between devices, deliver(): lax.all_to_all(outbound, 'expert', split_axis=0, concat_axis=0, tiled=True)  16.2 us
    all_to_all x1, waiting for transfers between devices, deliver(): lax.all_to_all(outbound, 'expert', split_axis=0, concat_axis=0, tiled=True)  15.4 us
  transfers between devices with their start and end apart: 3, of which 3 were waited for; matrix products, arithmetic and copies ran while one was open for 5% of the time, Pallas kernels for 0%

profile of v1, /device:TPU:1, one launch (start us, length us, event | category | flops | bytes accessed | tf_op | source)
XLA Modules:
  0.0 188.1 jit_solution(12492831920035731776)
XLA Ops:
  7.2 0.8 copy.34
  8.1 0.8 copy.36
  9.0 0.2 reduce_window_sum.11
  9.6 1.0 convolution_convert_fusion.7
  10.7 1.1 convolution_convert_fusion.6
  11.9 0.7 pad_maximum_fusion
  12.6 38.8 %all_to_all.10 = bf16[128,2,2,512]{3,1,2,0:T(2,128)(2,1)S(1)} all-to-all(bf16[128,2,2,512]{3,1,2,0:T(2,128)(2,1)S(1)} %pad_maximum_fusion), channel_id=1, replica_groups=mesh['dp'=4,'expert'=128] {'expert'}, dimensions={0} | all-to-all | bytes 1048576 | tf_op jit(solution)/shard_map/all_to_all | solution.py:20
  51.4 0.4 copy.39
  51.8 0.7 fusion.40
  52.6 0.3 copy-done.2
  53.0 1.2 convolution_convert_fusion.4
  54.2 1.1 convolution_convert_fusion.5
  55.4 1.2 convolution_convert_fusion.3
  56.5 21.8 %all-gather.3.cloned.1.call-done = bf16[1024,768]{1,0:T(8,128)(2,1)} async-done(((bf16[256,768]{1,0:T(8,128)(2,1)}), bf16[1024,768]{1,0:T(8,128)(2,1)}) %all-gather.3.cloned.1.call-update) | async-done | bytes 1572880 | tf_op jit(solution)/shard_map/all_gather | solution.py:26
  78.4 1.8 reduce_sum.45
  80.2 54.6 %all-reduce.3.cloned.1.call-done = (bf16[256,768]{1,0:T(8,128)(2,1)}, bf16[256,768]{1,0:T(8,128)(2,1)}) async-done(((bf16[256,768]{1,0:T(8,128)(2,1)}, bf16[256,768]{1,0:T(8,128)(2,1)}), (bf16[256,768]{1,0:T(8,128)(2,1)}, bf16[256,768]{1,0:T(8,128)(2,1)})) %all-reduce.3.cloned.1.call-update) | async-done | bytes 786448 | tf_op jit(solution)/shard_map/psum | solution.py:69
  134.8 2.2 %convolution_convert_fusion.8 = bf16[256,512]{1,0:T(8,128)(2,1)} fusion(bf16[1,768,512]{2,1,0:T(8,128)(2,1)S(1)} %copy-done, bf16[256,768]{1,0:T(8,128)(2,1)S(1)} %reduce_sum.45, bf16[256,768]{1,0:T(8,128)(2,1)} %get-tuple-element.8), kind=kOutput, calls=%fused_computation.13 | convolution fusion | flops 203030528 | bytes 1835008 | tf_op jit(solution)/shard_map/dot_general | solution.py:72
  137.0 0.4 fusion.7
  137.4 1.1 stack.21
  138.4 0.4 fusion.17
  138.8 0.7 copy-done.3
  139.8 0.4 fusion.3
  140.3 1.5 pad_maximum_fusion.1
  141.8 16.2 %all-to-all-start.1 = ((bf16[128,2,2,512]{3,1,2,0:T(2,128)(2,1)}), bf16[128,2,2,512]{3,1,2,0:T(2,128)(2,1)S(1)}, u32[]{:S(2)}, u32[]{:S(2)}) async-start(bf16[128,2,2,512]{3,1,2,0:T(2,128)(2,1)} %pad_maximum_fusion.1), calls=%async_computation.1 | async-start | bytes 1048576 | tf_op jit(solution)/shard_map/all_to_all | solution.py:20
  158.0 2.5 %fusion.1 = bf16[1,768,512]{2,1,0:T(8,128)(2,1)} fusion(bf16[256,1,512]{2,0,1:T(8,128)(2,1)S(1)} %copy.43, bf16[256,768]{1,0:T(8,128)(2,1)} %get-tuple-element.7, bf16[256,768]{1,0:T(8,128)(2,1)} %get-tuple-element.8), kind=kOutput, calls=%fused_computation.4 | convolution fusion | flops 203292672 | bytes 1835008 | tf_op jit(solution)/shard_map/dot_general | solution.py:80
  160.5 1.3 fusion
  161.8 1.4 fusion.2
  163.1 15.4 %all-to-all-done.1 = bf16[128,2,2,512]{3,1,2,0:T(2,128)(2,1)S(1)} async-done(((bf16[128,2,2,512]{3,1,2,0:T(2,128)(2,1)}), bf16[128,2,2,512]{3,1,2,0:T(2,128)(2,1)S(1)}, u32[]{:S(2)}, u32[]{:S(2)}) %all-to-all-start.1) | async-done | bytes 524320 | tf_op jit(solution)/shard_map/all_to_all | solution.py:20
  178.5 0.4 copy.42
  179.0 0.7 fusion.39
  179.7 0.8 convolution_convert_fusion.9
  180.5 0.8 convolution_convert_fusion.10
  (30 shorter events, 1.3 us)
Async XLA Ops:
  7.2 48.2 %copy-start = (bf16[1,768,512]{2,1,0:T(8,128)(2,1)S(1)}, bf16[1,768,512]{2,1,0:T(8,128)(2,1)}, u32[]{:S(2)}) copy-start(bf16[1,768,512]{2,1,0:T(8,128)(2,1)} %param.13) | copy-start | bytes 2359300
  7.2 71.2 %all-gather.3.cloned.1.call-start = ((), (), s32[]{:S(2)}) async-start(), calls=%async_computation.2 | async-start | bytes 1966080 | tf_op jit(solution)/shard_map/all_gather | solution.py:26
  51.8 1.1 copy-start.2
  52.6 1.6 copy-start.1
  54.1 80.6 %all-reduce.3.cloned.1.call-start = ((), (), s32[]{:S(2)}) async-start(), calls=%async_computation.3 | async-start | bytes 1572864 | tf_op jit(solution)/shard_map/psum | solution.py:69
  134.8 2.2 %copy-start.4 = (bf16[256,768]{1,0:T(8,128)(2,1)S(1)}, bf16[256,768]{1,0:T(8,128)(2,1)}, u32[]{:S(2)}) copy-start(bf16[256,768]{1,0:T(8,128)(2,1)} %get-tuple-element.8) | copy-start | bytes 1179652
  134.8 2.2 %copy-start.7 = (bf16[256,768]{1,0:T(8,128)(2,1)S(1)}, bf16[256,768]{1,0:T(8,128)(2,1)}, u32[]{:S(2)}) copy-start(bf16[256,768]{1,0:T(8,128)(2,1)} %get-tuple-element.7) | copy-start | bytes 1179652
  138.4 1.1 copy-start.3
  138.4 1.2 copy-start.5
  138.4 1.3 copy-start.8
  141.8 36.8 %all-to-all-start.1 = ((bf16[128,2,2,512]{3,1,2,0:T(2,128)(2,1)}), bf16[128,2,2,512]{3,1,2,0:T(2,128)(2,1)S(1)}, u32[]{:S(2)}, u32[]{:S(2)}) async-start(bf16[128,2,2,512]{3,1,2,0:T(2,128)(2,1)} %pad_maximum_fusion.1), calls=%async_computation.1 | async-start | bytes 1048576 | tf_op jit(solution)/shard_map/all_to_all | solution.py:20
  158.0 3.8 %copy-start.6 = (bf16[256,768]{1,0:T(8,128)(2,1)S(1)}, bf16[256,768]{1,0:T(8,128)(2,1)}, u32[]{:S(2)}) copy-start(bf16[256,768]{1,0:T(8,128)(2,1)} %get-tuple-element.8) | copy-start | bytes 1179652
Sparse Core Ops, SparseCore 0:
  54.3 24.0 all-gather.2
  81.3 53.4 all-reduce.2
